TPU v7x, 32 devices: a whole 2x2x4 slice. The times are simulated.
32 devices in a mesh: fsdp: 8 (over z, y), rep: 4 (over x, core).
Axes of the slice: x: 2, y: 2, z: 4, core: 2. Of those that a mesh axis runs over, the one named last changes fastest.
Arguments:
- tokens: bfloat16 [64, 512, 768], P(('fsdp', 'rep')), may hold values from -6 to 6
- page_ids: int32 [64, 512], P(('fsdp', 'rep')), may hold values from 0 to 7, never falling along the last dimension, each value on 1 to 128 neighbouring positions
- box_coords: int32 [8, 64, 512], P(None, ('fsdp', 'rep')), may hold values from 0 to 1000
- w_qkv: bfloat16 [768, 2304], P('fsdp'), may hold values from -0.3125 to 0.3125
- b_qkv: bfloat16 [2304], P('fsdp'), may hold values from -3 to 3
- w_pos: bfloat16 [24576], P('fsdp'), may hold values from -0.75 to 0.75
- w_out: bfloat16 [768, 768], P('fsdp'), may hold values from -0.875 to 0.875
- b_out: bfloat16 [768], P('fsdp'), may hold values from -3 to 3
- gain_one: bfloat16 [768], P('fsdp'), may hold values from 0.5 to 1.5
- shift_one: bfloat16 [768], P('fsdp'), may hold values from -3 to 3
- w_up: bfloat16 [768, 3072], P('fsdp'), may hold values from -0.21875 to 0.21875
- b_up: bfloat16 [3072], P('fsdp'), may hold values from -3 to 3
- w_down: bfloat16 [3072, 768], P('fsdp'), may hold values from -0.109375 to 0.109375
- b_down: bfloat16 [768], P('fsdp'), may hold values from -3 to 3
- gain_two: bfloat16 [768], P('fsdp'), may hold values from 0.5 to 1.5
- shift_two: bfloat16 [768], P('fsdp'), may hold values from -3 to 3
- cotangent: bfloat16 [64, 512, 768], P(('fsdp', 'rep')), may hold values from -6 to 6
Outputs:
- layer_out: bfloat16 [64, 512, 768], P(('fsdp', 'rep'))
- grad_tokens: bfloat16 [64, 512, 768], P(('fsdp', 'rep'))
- grad_w_qkv: float32 [768, 2304], P('fsdp')
- grad_b_qkv: float32 [2304], P('fsdp')
- grad_w_pos: float32 [24576], P('fsdp')
- grad_w_out: float32 [768, 768], P('fsdp')
- grad_b_out: float32 [768], P('fsdp')
- grad_gain_one: float32 [768], P('fsdp')
- grad_shift_one: float32 [768], P('fsdp')
- grad_w_up: float32 [768, 3072], P('fsdp')
- grad_b_up: float32 [3072], P('fsdp')
- grad_w_down: float32 [3072, 768], P('fsdp')
- grad_b_down: float32 [768], P('fsdp')
- grad_gain_two: float32 [768], P('fsdp')
- grad_shift_two: float32 [768], P('fsdp')
Inputs may be any that keep to these rules, and one draw needn't show every extreme that they name: `page_ids`: within a row page ids never fall; every page holds 1 to 128 tokens, and one page of every row exactly 128.
All inputs are finite; a program needn't handle non-finite values.
Results may differ from a plain program's by a relative error of at most 0.017.
Values may be sent and summed in bfloat16 or wider, within the bound.
No kernel may reach another device: no remote copies, remote signals or barrier semaphores. Data moves between devices by JAX's collectives and lax.ppermute only.
A program may use at most 256 MiB of HBM per device.

v0:
```python
import math
import jax
import jax.numpy as jnp
from jax import lax
from jax.sharding import PartitionSpec as P

HEADS = 12
HD = 64
PE = 192
norm_eps = 1e-12


def layer_norm(values, gain, shift):
    center = jnp.mean(values, axis=-1, keepdims=True)
    offset = values - center
    spread = jnp.mean(offset * offset, axis=-1, keepdims=True)
    return offset * lax.rsqrt(spread + norm_eps) * gain + shift


def gelu_exact(values):
    return jax.nn.gelu(values, approximate=False)


def pair_swap(matrix):
    return matrix.reshape(PE // 2, 2, matrix.shape[-1])[:, ::-1].reshape(PE, matrix.shape[-1])


def row_scores(left_side, right_side, row_pages, score_scale):
    logits = jnp.einsum("hie,hje->hij", left_side, right_side, preferred_element_type=jnp.float32)
    same_page = row_pages[:, None] == row_pages[None, :]
    return jnp.where(same_page[None], logits * score_scale, -1e30)


def attend_row(left_side, right_side, value_heads, row_pages, score_scale):
    scores = row_scores(left_side, right_side, row_pages, score_scale)
    row_max = jnp.max(scores, axis=-1, keepdims=True)
    row_total = jnp.sum(jnp.exp(scores - row_max), axis=-1, keepdims=True)
    log_total = row_max + jnp.log(row_total)
    probs_low = jnp.exp(scores - log_total).astype(jnp.bfloat16)
    context = jnp.einsum("hij,hjd->hid", probs_low, value_heads, preferred_element_type=jnp.float32)
    return (context, log_total)


def attend_back(left_side, right_side, value_heads, row_pages, log_total, grad_ctx, score_scale):
    scores = row_scores(left_side, right_side, row_pages, score_scale)
    attn_probs = jnp.exp(scores - log_total)
    probs_low = attn_probs.astype(jnp.bfloat16)
    grad_probs = jnp.einsum(
        "hid,hjd->hij", grad_ctx, value_heads, preferred_element_type=jnp.float32
    )
    inner_sum = jnp.sum(grad_probs * attn_probs, axis=-1, keepdims=True)
    grad_logits = (attn_probs * (grad_probs - inner_sum) * score_scale).astype(jnp.bfloat16)
    grad_left = jnp.einsum(
        "hij,hje->hie", grad_logits, right_side, preferred_element_type=jnp.float32
    )
    grad_right = jnp.einsum(
        "hij,hie->hje", grad_logits, left_side, preferred_element_type=jnp.float32
    )
    grad_values = jnp.einsum(
        "hij,hid->hjd", probs_low, grad_ctx, preferred_element_type=jnp.float32
    )
    return (grad_left, grad_right, grad_values)


def body(
    tokens,
    page_ids,
    box_coords,
    w_qkv,
    b_qkv,
    w_pos,
    w_out,
    b_out,
    gain_one,
    shift_one,
    w_up,
    b_up,
    w_down,
    b_down,
    gain_two,
    shift_two,
    cotangent,
):
    row_count, seq_len, model_width = tokens.shape
    tok_count = row_count * seq_len
    score_scale = 1.0 / math.sqrt(HD + 2 * PE)
    shards = (
        w_qkv,
        w_out,
        w_up,
        w_down,
        b_qkv,
        w_pos,
        b_out,
        gain_one,
        shift_one,
        b_up,
        b_down,
        gain_two,
        shift_two,
    )
    gathered = (
        lax.all_gather(shards[0], "fsdp", axis=0, tiled=True),
        lax.all_gather(shards[1], "fsdp", axis=0, tiled=True),
        lax.all_gather(shards[2], "fsdp", axis=0, tiled=True),
        lax.all_gather(shards[3], "fsdp", axis=0, tiled=True),
        lax.all_gather(shards[4], "fsdp", axis=0, tiled=True),
        lax.all_gather(shards[5], "fsdp", axis=0, tiled=True),
        lax.all_gather(shards[6], "fsdp", axis=0, tiled=True),
        lax.all_gather(shards[7], "fsdp", axis=0, tiled=True),
        lax.all_gather(shards[8], "fsdp", axis=0, tiled=True),
        lax.all_gather(shards[9], "fsdp", axis=0, tiled=True),
        lax.all_gather(shards[10], "fsdp", axis=0, tiled=True),
        lax.all_gather(shards[11], "fsdp", axis=0, tiled=True),
        lax.all_gather(shards[12], "fsdp", axis=0, tiled=True),
    )
    (
        full_qkv,
        full_out,
        full_up,
        full_down,
        bias_qkv,
        pos_flat,
        bias_out,
        gain_first,
        shift_first,
        bias_up,
        bias_down,
        gain_second,
        shift_second,
    ) = gathered
    pos_all = pos_flat.reshape(2, PE, HD)

    def to_heads(flat_in):
        return flat_in.reshape(row_count, seq_len, HEADS, HD).transpose(0, 2, 1, 3)

    def from_heads(head_in):
        return head_in.transpose(0, 2, 1, 3).reshape(tok_count, model_width)

    flat_rows = tokens.reshape(tok_count, model_width)
    qkv_low = (
        jnp.dot(flat_rows, full_qkv, preferred_element_type=jnp.float32)
        + bias_qkv.astype(jnp.float32)
    ).astype(jnp.bfloat16)
    query_heads = to_heads(qkv_low[:, :model_width])
    key_heads = to_heads(qkv_low[:, model_width : 2 * model_width])
    value_heads = to_heads(qkv_low[:, 2 * model_width :])
    freq_count = PE // 16
    freq_vals = jnp.exp(
        jnp.arange(freq_count).astype(jnp.float32) * (-math.log(10000.0) / freq_count)
    )
    angles = jnp.moveaxis(box_coords, 0, -1).astype(jnp.float32)[..., None] * freq_vals
    sin_vals = jnp.sin(angles)
    cos_vals = jnp.cos(angles)
    feat_shape = (row_count, 1, seq_len, PE)
    box_feats = jnp.stack([sin_vals, cos_vals], axis=-1).reshape(feat_shape)
    sin_rep = jnp.stack([sin_vals, sin_vals], axis=-1).reshape(feat_shape)
    cos_sign = jnp.stack([-cos_vals, cos_vals], axis=-1).reshape(feat_shape)
    comb_query = jnp.concatenate([pos_all[1], pair_swap(pos_all[1])], axis=0)
    comb_key = jnp.concatenate([pos_all[0], pair_swap(pos_all[0])], axis=0)
    query_pos = jnp.einsum(
        "rhld,fd->rhlf", query_heads, comb_query, preferred_element_type=jnp.float32
    )
    key_pos = jnp.einsum("rhld,fd->rhlf", key_heads, comb_key, preferred_element_type=jnp.float32)
    turned_query = query_pos[..., PE:] * sin_rep + query_pos[..., :PE] * cos_sign
    turned_key = key_pos[..., PE:] * sin_rep + key_pos[..., :PE] * cos_sign
    feats_heads = jnp.broadcast_to(box_feats.astype(jnp.bfloat16), (row_count, HEADS, seq_len, PE))
    left_all = jnp.concatenate(
        [query_heads, turned_query.astype(jnp.bfloat16), feats_heads], axis=-1
    )
    right_all = jnp.concatenate([key_heads, feats_heads, turned_key.astype(jnp.bfloat16)], axis=-1)

    def row_forward(inputs):
        left_side, right_side, row_values, row_pages = inputs
        return attend_row(left_side, right_side, row_values, row_pages, score_scale)

    ctx_rows, total_rows = lax.map(row_forward, (left_all, right_all, value_heads, page_ids))
    ctx_low = from_heads(ctx_rows).astype(jnp.bfloat16)
    attn_out = jnp.dot(ctx_low, full_out, preferred_element_type=jnp.float32) + bias_out.astype(
        jnp.float32
    )
    first_sum = flat_rows.astype(jnp.float32) + attn_out
    hidden, norm_back_one = jax.vjp(
        layer_norm, first_sum, gain_first.astype(jnp.float32), shift_first.astype(jnp.float32)
    )
    hidden_low = hidden.astype(jnp.bfloat16)
    up_proj = jnp.dot(hidden_low, full_up, preferred_element_type=jnp.float32) + bias_up.astype(
        jnp.float32
    )
    activated, gelu_back = jax.vjp(gelu_exact, up_proj)
    act_low = activated.astype(jnp.bfloat16)
    ffn_out = jnp.dot(act_low, full_down, preferred_element_type=jnp.float32) + bias_down.astype(
        jnp.float32
    )
    result, norm_back_two = jax.vjp(
        layer_norm,
        hidden + ffn_out,
        gain_second.astype(jnp.float32),
        shift_second.astype(jnp.float32),
    )
    layer_out = result.reshape(row_count, seq_len, model_width).astype(jnp.bfloat16)
    again = (
        lax.all_gather(shards[0], "fsdp", axis=0, tiled=True),
        lax.all_gather(shards[1], "fsdp", axis=0, tiled=True),
        lax.all_gather(shards[2], "fsdp", axis=0, tiled=True),
        lax.all_gather(shards[3], "fsdp", axis=0, tiled=True),
        lax.all_gather(shards[4], "fsdp", axis=0, tiled=True),
        lax.all_gather(shards[5], "fsdp", axis=0, tiled=True),
        lax.all_gather(shards[6], "fsdp", axis=0, tiled=True),
        lax.all_gather(shards[7], "fsdp", axis=0, tiled=True),
        lax.all_gather(shards[8], "fsdp", axis=0, tiled=True),
        lax.all_gather(shards[9], "fsdp", axis=0, tiled=True),
        lax.all_gather(shards[10], "fsdp", axis=0, tiled=True),
        lax.all_gather(shards[11], "fsdp", axis=0, tiled=True),
        lax.all_gather(shards[12], "fsdp", axis=0, tiled=True),
    )
    back_qkv, back_out, back_up, back_down = (again[0], again[1], again[2], again[3])
    back_pos = again[5].reshape(2, PE, HD).astype(jnp.float32)
    back_comb_query = jnp.concatenate([back_pos[1], pair_swap(back_pos[1])], axis=0)
    back_comb_key = jnp.concatenate([back_pos[0], pair_swap(back_pos[0])], axis=0)
    grad_result = cotangent.reshape(tok_count, model_width).astype(jnp.float32)
    grad_second, grad_gain_two, grad_shift_two = norm_back_two(grad_result)
    grad_ffn = grad_second.astype(jnp.bfloat16)
    grad_w_down = jnp.einsum("nf,nd->fd", act_low, grad_ffn, preferred_element_type=jnp.float32)
    grad_b_down = jnp.sum(grad_ffn.astype(jnp.float32), axis=0)
    grad_act = jnp.einsum("nd,fd->nf", grad_ffn, back_down, preferred_element_type=jnp.float32)
    grad_up = gelu_back(grad_act)[0].astype(jnp.bfloat16)
    grad_w_up = jnp.einsum("nd,nf->df", hidden_low, grad_up, preferred_element_type=jnp.float32)
    grad_b_up = jnp.sum(grad_up.astype(jnp.float32), axis=0)
    grad_hidden = grad_second + jnp.einsum(
        "nf,df->nd", grad_up, back_up, preferred_element_type=jnp.float32
    )
    grad_first, grad_gain_one, grad_shift_one = norm_back_one(grad_hidden)
    grad_attn = grad_first.astype(jnp.bfloat16)
    grad_w_out = jnp.einsum("nc,nd->cd", ctx_low, grad_attn, preferred_element_type=jnp.float32)
    grad_b_out = jnp.sum(grad_attn.astype(jnp.float32), axis=0)
    grad_ctx = jnp.einsum(
        "nd,cd->nc", grad_attn, back_out, preferred_element_type=jnp.float32
    ).astype(jnp.bfloat16)

    def row_backward(inputs):
        left_side, right_side, row_values, row_pages, log_total, row_grad = inputs
        return attend_back(
            left_side, right_side, row_values, row_pages, log_total, row_grad, score_scale
        )

    grad_left, grad_right, grad_values = lax.map(
        row_backward, (left_all, right_all, value_heads, page_ids, total_rows, to_heads(grad_ctx))
    )
    grad_turn_query = grad_left[..., HD : HD + PE]
    grad_turn_key = grad_right[..., HD + PE :]
    grad_comb_q = jnp.concatenate([grad_turn_query * cos_sign, grad_turn_query * sin_rep], axis=-1)
    grad_comb_k = jnp.concatenate([grad_turn_key * cos_sign, grad_turn_key * sin_rep], axis=-1)
    grad_query = grad_left[..., :HD] + jnp.einsum(
        "rhlf,fd->rhld", grad_comb_q, back_comb_query, precision=lax.Precision.HIGHEST
    )
    grad_keys = grad_right[..., :HD] + jnp.einsum(
        "rhlf,fd->rhld", grad_comb_k, back_comb_key, precision=lax.Precision.HIGHEST
    )
    comb_from_query = jnp.einsum(
        "rhld,rhlf->fd",
        query_heads.astype(jnp.float32),
        grad_comb_q,
        precision=lax.Precision.HIGHEST,
    )
    comb_from_key = jnp.einsum(
        "rhld,rhlf->fd", key_heads.astype(jnp.float32), grad_comb_k, precision=lax.Precision.HIGHEST
    )
    grad_pos_key = comb_from_query[:PE] + pair_swap(comb_from_query[PE:])
    grad_pos_query = comb_from_key[:PE] + pair_swap(comb_from_key[PE:])
    grad_w_pos = jnp.stack([grad_pos_query, grad_pos_key]).reshape(2 * PE * HD)
    grad_qkv = jnp.concatenate(
        [from_heads(grad_query), from_heads(grad_keys), from_heads(grad_values)], axis=1
    ).astype(jnp.bfloat16)
    grad_w_qkv = jnp.einsum("nd,ne->de", flat_rows, grad_qkv, preferred_element_type=jnp.float32)
    grad_b_qkv = jnp.sum(grad_qkv.astype(jnp.float32), axis=0)
    grad_input = grad_first + jnp.einsum(
        "ne,de->nd", grad_qkv, back_qkv, preferred_element_type=jnp.float32
    )
    grad_tokens = grad_input.reshape(row_count, seq_len, model_width).astype(jnp.bfloat16)
    partials = (
        grad_w_qkv,
        grad_w_out,
        grad_w_up,
        grad_w_down,
        grad_b_qkv,
        grad_w_pos,
        grad_b_out,
        grad_gain_one,
        grad_shift_one,
        grad_b_up,
        grad_b_down,
        grad_gain_two,
        grad_shift_two,
    )
    shard_sums = (
        lax.psum_scatter(partials[0], "fsdp", scatter_dimension=0, tiled=True),
        lax.psum_scatter(partials[1], "fsdp", scatter_dimension=0, tiled=True),
        lax.psum_scatter(partials[2], "fsdp", scatter_dimension=0, tiled=True),
        lax.psum_scatter(partials[3], "fsdp", scatter_dimension=0, tiled=True),
        lax.psum_scatter(partials[4], "fsdp", scatter_dimension=0, tiled=True),
        lax.psum_scatter(partials[5], "fsdp", scatter_dimension=0, tiled=True),
        lax.psum_scatter(partials[6], "fsdp", scatter_dimension=0, tiled=True),
        lax.psum_scatter(partials[7], "fsdp", scatter_dimension=0, tiled=True),
        lax.psum_scatter(partials[8], "fsdp", scatter_dimension=0, tiled=True),
        lax.psum_scatter(partials[9], "fsdp", scatter_dimension=0, tiled=True),
        lax.psum_scatter(partials[10], "fsdp", scatter_dimension=0, tiled=True),
        lax.psum_scatter(partials[11], "fsdp", scatter_dimension=0, tiled=True),
        lax.psum_scatter(partials[12], "fsdp", scatter_dimension=0, tiled=True),
    )
    totals = (
        lax.psum(shard_sums[0].astype(jnp.bfloat16), "rep").astype(jnp.float32),
        lax.psum(shard_sums[1].astype(jnp.bfloat16), "rep").astype(jnp.float32),
        lax.psum(shard_sums[2].astype(jnp.bfloat16), "rep").astype(jnp.float32),
        lax.psum(shard_sums[3].astype(jnp.bfloat16), "rep").astype(jnp.float32),
        lax.psum(shard_sums[4].astype(jnp.bfloat16), "rep").astype(jnp.float32),
        lax.psum(shard_sums[5].astype(jnp.bfloat16), "rep").astype(jnp.float32),
        lax.psum(shard_sums[6].astype(jnp.bfloat16), "rep").astype(jnp.float32),
        lax.psum(shard_sums[7].astype(jnp.bfloat16), "rep").astype(jnp.float32),
        lax.psum(shard_sums[8].astype(jnp.bfloat16), "rep").astype(jnp.float32),
        lax.psum(shard_sums[9].astype(jnp.bfloat16), "rep").astype(jnp.float32),
        lax.psum(shard_sums[10].astype(jnp.bfloat16), "rep").astype(jnp.float32),
        lax.psum(shard_sums[11].astype(jnp.bfloat16), "rep").astype(jnp.float32),
        lax.psum(shard_sums[12].astype(jnp.bfloat16), "rep").astype(jnp.float32),
    )
    (
        sum_w_qkv,
        sum_w_out,
        sum_w_up,
        sum_w_down,
        sum_b_qkv,
        sum_w_pos,
        sum_b_out,
        sum_gain_one,
        sum_shift_one,
        sum_b_up,
        sum_b_down,
        sum_gain_two,
        sum_shift_two,
    ) = totals
    return (
        layer_out,
        grad_tokens,
        sum_w_qkv,
        sum_b_qkv,
        sum_w_pos,
        sum_w_out,
        sum_b_out,
        sum_gain_one,
        sum_shift_one,
        sum_w_up,
        sum_b_up,
        sum_w_down,
        sum_b_down,
        sum_gain_two,
        sum_shift_two,
    )


def solution(mesh):
    in_specs = (
        P(("fsdp", "rep"), None, None),
        P(("fsdp", "rep"), None),
        P(None, ("fsdp", "rep"), None),
        P("fsdp", None),
        P("fsdp"),
        P("fsdp"),
        P("fsdp", None),
        P("fsdp"),
        P("fsdp"),
        P("fsdp"),
        P("fsdp", None),
        P("fsdp"),
        P("fsdp", None),
        P("fsdp"),
        P("fsdp"),
        P("fsdp"),
        P(("fsdp", "rep"), None, None),
    )
    out_specs = (
        P(("fsdp", "rep"), None, None),
        P(("fsdp", "rep"), None, None),
        P("fsdp", None),
        P("fsdp"),
        P("fsdp"),
        P("fsdp", None),
        P("fsdp"),
        P("fsdp"),
        P("fsdp"),
        P("fsdp", None),
        P("fsdp"),
        P("fsdp", None),
        P("fsdp"),
        P("fsdp"),
        P("fsdp"),
    )
    return jax.shard_map(body, mesh=mesh, in_specs=in_specs, out_specs=out_specs, check_vma=False)
```

profile of v0, /device:TPU:0, one launch (start us, length us, event | category | flops | bytes accessed | tf_op | source)
XLA Modules:
  0.0 1125.1 jit_solution(646275522644799636)
XLA Ops:
  10.0 33.1 %all_gather.46 = bf16[24576]{0:T(1024)(128)(2,1)S(1)} all-gather(bf16[3072]{0:T(1024)(128)(2,1)} %param.26), channel_id=1, replica_groups=mesh['fsdp'=8,'rep'=4] {'fsdp'}, dimensions={0}, use_global_device_ids=true | all-gather | bytes 55296 | tf_op jit(solution)/shard_map/all_gather | solution.py:108
  53.1 38.1 %all-reduce.17 = (bf16[2304]{0:T(1024)(128)(2,1)S(1)}, bf16[768]{0:T(1024)(128)(2,1)S(1)}, bf16[768]{0:T(1024)(128)(2,1)S(1)}, bf16[768]{0:T(1024)(128)(2,1)S(1)...) all-reduce(bf16[2304]{0:T(1024)(128)(2,1)S(1)} %dynamic-update-slic, ...), channel_id=1, replica_groups=mesh['fsdp'=8,'rep'=4] {'fsdp'}, use_global_device_ids=true, to_apply=%add | all-reduce | flops 6912 | bytes 27648
  94.2 26.3 %all-gather = bf16[8,1,384]{2,1,0:T(2,128)(2,1)S(1)} all-gather(bf16[1,1,384]{2,1,0:T(2,128)(2,1)S(1)} %reshape.371), channel_id=1, replica_groups=mesh['fsdp'=8,'rep'=4] {'fsdp'}, dimensions={0}, use_global_device_ids=true | all-gather | bytes 6912 | tf_op jit(solution)/shard_map/all_gather | solution.py:112
  133.9 6.6 add_convert_fusion.1
  143.2 2.4 reshape.337
  147.3 2.6 copy.177
  149.9 3.9 reshape.335
  153.8 2.6 copy.166
  156.4 3.9 reshape.333
  160.3 4.4 copy_bitcast_fusion
  164.7 2.8 fusion.131
  167.6 8.1 fusion.134
  175.7 13.3 %fusion.98 = (bf16[2,12,512,192]{2,3,1,0:T(8,128)(2,1)}, bf16[2,12,512,192]{2,3,1,0:T(8,128)(2,1)}) fusion(f32[2,12,512,384]{2,3,1,0:T(8,128)} %fusion.134, f32[2,512,192]{1,2,0:T(8,128)} %copy.174, f32[2,512,192]{1,2,0:T(8,128)} %copy.172, f32[2,12,512,384]{2,3,1,0:T(8,128)S(1)} %fusion.131), kind=kLoop, calls=%fused_computation.103 | loop fusion | flops 18874368 | bytes 48758784 | tf_op jit(solution)/shard_map/convert_element_type | solution.py:171
  191.4 11.2 pad_maximum_fusion.3
  203.8 50.8 %while.26 = (s32[]{:T(128)}, bf16[2,12,512,64]{2,3,1,0:T(8,128)(2,1)}, f32[2,12,512,1]{2,1,3,0:T(8,128)}, s32[2,512]{1,0:T(2,128)S(1)}, bf16[2,12,512,448]{2,3,1...) while((s32[]{:T(128)}, ...), condition=%wide.region_3.4_spmd, body=%wide.region_0.3_spmd.sunk | while | flops 3256084480 | bytes 102719608 | solution.py:177
  204.2 12.8 %fusion.195 = (f32[12,512]{1,0:T(8,128)S(1)}, f32[12,512,512]{1,2,0:T(8,128)}) fusion(pred[512,512]{0,1:T(8,128)(4,1)S(1)} %broadcast_compare_fusion.4, bf16[2,12,512,448]{2,3,1,0:T(8,128)(2,1)} %get-tuple-element.507, s32[]{:T(128)S(6)} %copy.269, bf16[2,12,512,448]{2,3,1,0:T(8,128)(2,1)} %get-tuple-element.506), kind=kOutput, calls=%fused_computation.3.clone.1 | convolution fusion | flops 2828003328 | bytes 23880704 | tf_op jit(solution)/shard_map/while/body/eval_jaxpr/hie,hje->hij/dot_general | solution.py:29
  217.0 7.3 exponential_reduce_fusion.2
  225.3 4.0 bitcast_dynamic-update-slice_fusion.11
  229.5 12.7 %fusion.195 = (f32[12,512]{1,0:T(8,128)S(1)}, f32[12,512,512]{1,2,0:T(8,128)}) fusion(pred[512,512]{0,1:T(8,128)(4,1)S(1)} %broadcast_compare_fusion.4, bf16[2,12,512,448]{2,3,1,0:T(8,128)(2,1)} %get-tuple-element.507, s32[]{:T(128)S(6)} %copy.269, bf16[2,12,512,448]{2,3,1,0:T(8,128)(2,1)} %get-tuple-element.506), kind=kOutput, calls=%fused_computation.3.clone.1 | convolution fusion | flops 2828003328 | bytes 23880704 | tf_op jit(solution)/shard_map/while/body/eval_jaxpr/hie,hje->hij/dot_general | solution.py:29
  242.2 7.3 exponential_reduce_fusion.2
  250.5 4.0 bitcast_dynamic-update-slice_fusion.11
  254.7 3.6 copy.183
  259.9 3.9 fusion.154
  264.4 36.4 %multiply_convert_fusion.1 = (bf16[1024,3072]{1,0:T(8,128)(2,1)}, f32[1024,3072]{1,0:T(8,128)}, f32[1024,3072]{1,0:T(8,128)}) fusion(f32[3072]{0:T(1024)S(1)} %bitcast.258, bf16[768,3072]{1,0:T(8,128)(2,1)} %all-gather.10.cloned.1.call-done, f32[1024,768]{1,0:T(8,128)S(1)} %get-tuple-element.363, f32[768]{0:T(1024)S(1)} %copy-done.37, ...), kind=kOutput, calls=%fused_computation.85 | convolution fusion | flops 5043388416 | bytes 39348224 | tf_op jit(solution)/shard_map/dot_general | solution.py:187
  300.8 9.4 fusion.155
  312.6 2.6 fusion.148
  317.2 19.0 %convert_reduce_fusion = (f32[3072]{0:T(1024)}, bf16[1024,3072]{1,0:T(8,128)(2,1)}) fusion(f32[1024,3072]{1,0:T(8,128)} %get-tuple-element.334, bf16[1024,768]{1,0:T(8,128)(2,1)} %get-tuple-element.326, bf16[3072,768]{1,0:T(8,128)(2,1)} %all-gather.12.cloned.1.call-done, f32[1024,3072]{1,0:T(8,128)} %get-tuple-element.364, f32[3072]{0:T(1024)S(1)} %bitcast.259), kind=kOutput, calls=%fused_computation.83 | convolution fusion | flops 4885312512 | bytes 37773312 | tf_op jit(solution)/shard_map/nd,fd->nf/dot_general | solution.py:226
  336.2 10.1 multiply_reduce_fusion.1
  350.4 2.8 fusion.156
  353.2 2.6 convolution_convert_fusion
  357.6 2.4 reshape.338
  363.1 155.6 %while.27 = (s32[]{:T(128)}, f32[2,12,512,448]{2,3,1,0:T(8,128)}, f32[2,12,512,448]{2,3,1,0:T(8,128)}, bf16[2,12,512,64]{2,3,1,0:T(8,128)(2,1)}, s32[2,512]{1,0:...) while((s32[]{:T(128)}, f32[2,12,512,448]{2,3,1,0:T(8,128)}, ...), condition=%wide.region_14.15_spmd, body=%wide.region_12.14_spmd.sunk | while | flops 9343087616 | bytes 188181648 | solution.py:247
  363.5 12.4 %fusion.207 = f32[12,512,512]{1,2,0:T(8,128)} fusion(bf16[2,12,512,448]{2,3,1,0:T(8,128)(2,1)} %get-tuple-element.538, s32[]{:T(128)S(6)} %copy.279, bf16[2,12,512,448]{2,3,1,0:T(8,128)(2,1)} %get-tuple-element.537), kind=kOutput, calls=%fused_computation.43.clone.1 | convolution fusion | flops 2818572288 | bytes 23593984 | tf_op jit(solution)/shard_map/while/body/eval_jaxpr/hie,hje->hij/dot_general | solution.py:29
  376.0 7.4 bitcast_dynamic-update-slice_fusion.14
  383.4 6.3 fusion.206
  389.7 27.8 %bitcast_dynamic-update-slice_fusion.13 = f32[2,12,512,448]{2,3,1,0:T(8,128)} fusion(f32[2,12,512,448]{2,3,1,0:T(8,128)} %get-tuple-element.523, s32[]{:T(128)S(6)} %copy.279, bf16[2,12,512,448]{2,3,1,0:T(8,128)(2,1)} %get-tuple-element.537, f32[12,512,512]{1,2,0:T(8,128)} %fusion.206, f32[12,512,512]{1,2,0:T(8,128)} %fusion.207, ...), kind=kOutput, calls=%fused_computation.27.clone.1 | convolution fusion | flops 2853181952 | bytes 67437568 | tf_op jit(solution)/shard_map/while/body/eval_jaxpr/hij,hie->hje/dot_general | solution.py:56
  417.5 23.7 %bitcast_dynamic-update-slice_fusion.12 = f32[2,12,512,448]{2,3,1,0:T(8,128)} fusion(f32[2,12,512,448]{2,3,1,0:T(8,128)} %get-tuple-element.522, s32[]{:T(128)S(6)} %copy.279, f32[12,512,512]{1,2,0:T(8,128)} %fusion.206, f32[12,512,512]{1,2,0:T(8,128)} %fusion.207, f32[12,512]{1,0:T(8,128)S(1)} %dynamic-slice_bitcast_fusion.2, ...), kind=kOutput, calls=%fused_computation.28.clone.1 | convolution fusion | flops 2853181952 | bytes 67437568 | tf_op jit(solution)/shard_map/while/body/eval_jaxpr/hij,hje->hie/dot_general | solution.py:53
  441.4 12.2 %fusion.207 = f32[12,512,512]{1,2,0:T(8,128)} fusion(bf16[2,12,512,448]{2,3,1,0:T(8,128)(2,1)} %get-tuple-element.538, s32[]{:T(128)S(6)} %copy.279, bf16[2,12,512,448]{2,3,1,0:T(8,128)(2,1)} %get-tuple-element.537), kind=kOutput, calls=%fused_computation.43.clone.1 | convolution fusion | flops 2818572288 | bytes 23593984 | tf_op jit(solution)/shard_map/while/body/eval_jaxpr/hie,hje->hij/dot_general | solution.py:29
  453.6 7.2 bitcast_dynamic-update-slice_fusion.14
  460.8 6.3 fusion.206
  467.2 27.8 %bitcast_dynamic-update-slice_fusion.13 = f32[2,12,512,448]{2,3,1,0:T(8,128)} fusion(f32[2,12,512,448]{2,3,1,0:T(8,128)} %get-tuple-element.523, s32[]{:T(128)S(6)} %copy.279, bf16[2,12,512,448]{2,3,1,0:T(8,128)(2,1)} %get-tuple-element.537, f32[12,512,512]{1,2,0:T(8,128)} %fusion.206, f32[12,512,512]{1,2,0:T(8,128)} %fusion.207, ...), kind=kOutput, calls=%fused_computation.27.clone.1 | convolution fusion | flops 2853181952 | bytes 67437568 | tf_op jit(solution)/shard_map/while/body/eval_jaxpr/hij,hie->hje/dot_general | solution.py:56
  494.9 23.6 %bitcast_dynamic-update-slice_fusion.12 = f32[2,12,512,448]{2,3,1,0:T(8,128)} fusion(f32[2,12,512,448]{2,3,1,0:T(8,128)} %get-tuple-element.522, s32[]{:T(128)S(6)} %copy.279, f32[12,512,512]{1,2,0:T(8,128)} %fusion.206, f32[12,512,512]{1,2,0:T(8,128)} %fusion.207, f32[12,512]{1,0:T(8,128)S(1)} %dynamic-slice_bitcast_fusion.2, ...), kind=kOutput, calls=%fused_computation.28.clone.1 | convolution fusion | flops 2853181952 | bytes 67437568 | tf_op jit(solution)/shard_map/while/body/eval_jaxpr/hij,hje->hie/dot_general | solution.py:53
  518.7 3.1 copy.195
  522.3 18.4 %slice_multiply_fusion.7 = (f32[2,12,512,192]{2,3,1,0:T(8,128)}, f32[2,12,512,192]{2,3,1,0:T(8,128)}, f32[2,12,512,192]{2,3,1,0:T(8,128)S(1)}, f32[2,12,512,192]{2,3,1,0:T(8,128)}) fusion(f32[2,12,512,448]{2,3,1,0:T(8,128)} %get-tuple-element.109, f32[2,512,192]{1,2,0:T(8,128)S(1)} %copy-done.17, f32[2,512,192]{1,2,0:T(8,128)S(1)} %copy-done.16, ...), kind=kLoop, calls=%fused_computation.114 | loop fusion | flops 9437184 | bytes 58195968 | tf_op jit(solution)/shard_map/mul | solution.py:252
  540.7 19.8 %fusion.110 = bf16[2,512,12,64]{1,3,2,0:T(8,128)(2,1)S(1)} fusion(f32[2,12,512,448]{2,3,1,0:T(8,128)} %get-tuple-element.109, f32[192,64]{0,1:T(8,128)S(1)} %copy-done.27, f32[192,64]{0,1:T(8,128)S(1)} %copy-done.28, f32[2,12,512,192]{2,3,1,0:T(8,128)} %get-tuple-element.340, f32[2,12,512,192]{2,3,1,0:T(8,128)} %get-tuple-element.339), kind=kOutput, calls=%fused_computation.151 | convolution fusion | flops 3630194688 | bytes 23691264 | tf_op jit(solution)/shard_map/rhlf,fd->rhld/dot_general | solution.py:254
  562.6 15.7 %fusion.111 = bf16[2,512,12,64]{1,3,2,0:T(8,128)(2,1)} fusion(f32[2,12,512,448]{2,3,1,0:T(8,128)} %get-tuple-element.110, f32[192,64]{0,1:T(8,128)S(1)} %copy-done.25, f32[192,64]{0,1:T(8,128)S(1)} %copy-done.26, f32[2,12,512,192]{2,3,1,0:T(8,128)S(1)} %get-tuple-element.347, f32[2,12,512,192]{2,3,1,0:T(8,128)} %get-tuple-element.348), kind=kOutput, calls=%fused_computation.152 | convolution fusion | flops 3630194688 | bytes 23691264 | tf_op jit(solution)/shard_map/rhlf,fd->rhld/dot_general | solution.py:257
  578.4 3.0 copy.194
  584.3 5.8 convolution_bitcast_fusion
  590.1 8.1 copy.224
  600.1 11.3 %fusion.143 = f32[768,3072]{1,0:T(8,128)} fusion(bf16[1024,3072]{1,0:T(8,128)(2,1)} %get-tuple-element.369, f32[1024,768]{1,0:T(8,128)S(1)} %copy-done.3, f32[768]{0:T(1024)S(1)} %copy-done.38, f32[768]{0:T(1024)S(1)} %copy-done.34, f32[1024]{0:T(1024)S(1)} %copy-done.24, f32[1024]{0:T(1024)S(1)} %copy-done.22), kind=kOutput, calls=%fused_computation.210 | convolution fusion | flops 4835770368 | bytes 18888704 | tf_op jit(solution)/shard_map/nd,nf->df/dot_general | solution.py:228
  612.8 10.4 fusion.157
  626.4 13.3 %fusion.117 = f32[384,64]{0,1:T(8,128)S(1)} fusion(bf16[2,512,12,64]{1,0,3,2:T(2,128)(2,1)S(1)} %copy-done.10, f32[2,12,512,192]{2,3,1,0:T(8,128)} %get-tuple-element.340, f32[2,12,512,192]{2,3,1,0:T(8,128)} %get-tuple-element.339), kind=kOutput, calls=%fused_computation.154 | convolution fusion | flops 3628597248 | bytes 20545536 | tf_op jit(solution)/shard_map/rhld,rhlf->fd/dot_general | solution.py:260
  640.3 13.0 %fusion.112 = f32[384,64]{0,1:T(8,128)S(1)} fusion(bf16[2,512,12,64]{1,0,3,2:T(2,128)(2,1)S(1)} %copy-done.8, f32[2,12,512,192]{2,3,1,0:T(8,128)} %copy-done.1, f32[2,12,512,192]{2,3,1,0:T(8,128)} %get-tuple-element.348), kind=kOutput, calls=%fused_computation.153 | convolution fusion | flops 3628597248 | bytes 20545536 | tf_op jit(solution)/shard_map/rhld,rhlf->fd/dot_general | solution.py:266
  654.2 3.2 convert_reduce_fusion.1
  657.4 35.1 %all-reduce.24 = (bf16[2304]{0:T(1024)(128)(2,1)S(1)}, bf16[24576]{0:T(1024)(128)(2,1)S(1)}, bf16[768]{0:T(1024)(128)(2,1)S(1)}, bf16[768]{0:T(1024)(128)(2,1)S(...) all-reduce(f32[2304]{0:T(1024)S(1)} %convert_reduce_fusion.1, ...), channel_id=3, replica_groups=mesh['fsdp'=8,'rep'=4] {'fsdp'}, use_global_device_ids=true, to_apply=%region_18.19.clone | all-reduce | flops 34560 | bytes 207360
  693.1 10.7 all-reduce.18
  710.3 18.5 %reduce-scatter.13.cloned.1.call-done = f32[96,2304]{1,0:T(8,128)} async-done(((f32[768,2304]{1,0:T(8,128)}), f32[96,2304]{1,0:T(8,128)}) %reduce-scatter.13.cloned.1.call-update) | async-done | bytes 884752
  728.8 2.2 copy.225
  731.0 162.6 %reduce-scatter.9.cloned.1.call-done = f32[96,3072]{1,0:T(8,128)} async-done(((f32[768,3072]{1,0:T(8,128)}), f32[96,3072]{1,0:T(8,128)}) %reduce-scatter.9.cloned.1.call-update) | async-done | bytes 1179664 | tf_op jit(solution)/shard_map/reduce_scatter | solution.py:299
  895.8 162.7 %reduce-scatter.11.cloned.1.call-done = f32[384,768]{1,0:T(8,128)} async-done(((f32[3072,768]{1,0:T(8,128)}), f32[384,768]{1,0:T(8,128)}) %reduce-scatter.11.cloned.1.call-update) | async-done | bytes 1179664 | tf_op jit(solution)/shard_map/reduce_scatter | solution.py:300
  1060.7 8.6 add_convert_fusion.2
  1069.3 40.8 %all-reduce.23.cloned.1.call-done = (bf16[96,2304]{0,1:T(8,128)(2,1)}, bf16[96,768]{1,0:T(8,128)(2,1)}, bf16[96,3072]{1,0:T(8,128)(2,1)}, bf16[384,768]{1,0:T(8,128)(2,1)}) async-done(((bf16[96,2304]{0,1:T(8,128)(2,1)}, bf16[96,768]{1,0:T(8,128)(2,1)}, bf16[96,3072]{1,0:T(8,128)(2,1)}, bf16[384,768]{1,0:T(8,128)(2,1)}), (bf16[96,2304]{0,1:T(8,128)(2,1)}, bf16[96,768]{1,0:T(8,128)(2,1)}, ...) | async-done | bytes 1769488 | tf_op jit(solution)/shard_map/psum | solution.py:312
  1110.1 2.2 copy.205
  1114.0 2.2 convert_element_type.261
  (273 shorter events, 79.4 us)
Async XLA Ops:
  7.2 126.7 %all-gather.6.cloned.1.call-start = ((), (), s32[]{:S(2)}) async-start(), calls=%async_computation.4 | async-start | bytes 3981312 | tf_op jit(solution)/shard_map/all_gather | solution.py:103
  7.9 252.0 %all-gather.8.cloned.1.call-start = ((), (), s32[]{:S(2)}) async-start(), calls=%async_computation.5 | async-start | bytes 1327104 | tf_op jit(solution)/shard_map/all_gather | solution.py:104
  8.7 255.6 %all-gather.10.cloned.1.call-start = ((), (), s32[]{:S(2)}) async-start(), calls=%async_computation.6 | async-start | bytes 5308416 | tf_op jit(solution)/shard_map/all_gather | solution.py:105
  9.4 291.4 %all-gather.12.cloned.1.call-start = ((), (), s32[]{:S(2)}) async-start(), calls=%async_computation.7 | async-start | bytes 5308416 | tf_op jit(solution)/shard_map/all_gather | solution.py:106
  10.0 698.7 %reduce-scatter.7.cloned.1.call-start = ((), (), s32[]{:S(2)}) async-start(), calls=%async_computation.8 | async-start | bytes 2654208 | tf_op jit(solution)/shard_map/reduce_scatter | solution.py:298
  128.4 5.5 copy-start.51
  153.8 10.9 copy-start.31
  153.8 10.9 copy-start.32
  160.3 4.4 copy-start.9
  164.7 2.9 copy-start.7
  164.7 2.9 copy-start.29
  164.7 2.9 copy-start.30
  189.0 2.3 copy-start.6
  191.4 12.5 %copy-start.35 = (s32[2,512]{1,0:T(2,128)S(1)}, s32[2,512]{1,0:T(2,128)}, u32[]{:S(2)}) copy-start(s32[2,512]{1,0:T(2,128)} %param.22) | copy-start | bytes 12292
  217.0 8.3 copy-start
  242.2 8.3 copy-start
  254.7 5.2 copy-start.4
  259.9 4.4 copy-start.33
  259.9 4.5 copy-start.37
  259.9 4.5 copy-start.47
  263.8 82.6 %copy-start.2 = (f32[1024,768]{1,0:T(8,128)}, f32[1024,768]{1,0:T(8,128)S(1)}, u32[]{:S(2)}) copy-start(f32[1024,768]{1,0:T(8,128)S(1)} %get-tuple-element.363) | copy-start | bytes 9437188
  263.8 82.6 %copy-start.21 = (f32[1024]{0:T(1024)}, f32[1024]{0:T(1024)S(1)}, u32[]{:S(2)}) copy-start(f32[1024]{0:T(1024)S(1)} %broadcast_multiply_fusion.1) | copy-start | bytes 12292
  264.3 82.1 %copy-start.23 = (f32[1024]{0:T(1024)}, f32[1024]{0:T(1024)S(1)}, u32[]{:S(2)}) copy-start(f32[1024]{0:T(1024)S(1)} %fusion.137) | copy-start | bytes 12292
  264.3 36.4 %copy-start.50 = (f32[768]{0:T(1024)S(1)}, f32[768]{0:T(1024)}, u32[]{:S(2)}) copy-start(f32[768]{0:T(1024)} %convert_element_type.230) | copy-start | bytes 9220
  300.8 10.0 copy-start.11
  300.8 10.0 copy-start.39
  310.2 2.3 copy-start.44
  346.3 4.0 copy-start.18
  347.8 1.6 copy-start.13
  347.8 5.4 copy-start.53
  347.9 2.5 copy-start.42
  355.8 7.3 copy-start.5
  355.8 7.3 copy-start.20
  355.8 7.3 copy-start.36
  361.7 367.1 %reduce-scatter.13.cloned.1.call-start = ((), (), s32[]{:S(2)}) async-start(), calls=%async_computation.11 | async-start | bytes 7962624
  518.7 3.6 copy-start.16
  518.7 3.6 copy-start.17
  522.3 18.4 %copy-start.27 = (f32[192,64]{0,1:T(8,128)S(1)}, f32[192,64]{0,1:T(8,128)}, u32[]{:S(2)}) copy-start(f32[192,64]{0,1:T(8,128)} %copy.188) | copy-start | bytes 147460
  522.3 18.4 %copy-start.28 = (f32[192,64]{0,1:T(8,128)S(1)}, f32[192,64]{0,1:T(8,128)}, u32[]{:S(2)}) copy-start(f32[192,64]{0,1:T(8,128)} %copy.187) | copy-start | bytes 147460
  540.7 21.9 %copy-start.1 = (f32[2,12,512,192]{2,3,1,0:T(8,128)}, f32[2,12,512,192]{2,3,1,0:T(8,128)S(1)}, u32[]{:S(2)}) copy-start(f32[2,12,512,192]{2,3,1,0:T(8,128)S(1)} %get-tuple-element.347) | copy-start | bytes 28311556
  560.5 2.1 copy-start.25
  560.6 2.1 copy-start.26
  581.4 3.0 copy-start.52
  582.2 2.1 copy-start.15
  598.2 1.9 copy-start.3
  598.2 1.9 copy-start.22
  598.2 1.9 copy-start.24
  598.2 1.9 copy-start.34
  598.2 1.9 copy-start.38
  598.3 295.4 %reduce-scatter.9.cloned.1.call-start = ((), (), s32[]{:S(2)}) async-start(), calls=%async_computation.9 | async-start | bytes 10616832 | tf_op jit(solution)/shard_map/reduce_scatter | solution.py:299
  611.4 1.4 copy-start.19
  611.4 447.1 %reduce-scatter.11.cloned.1.call-start = ((), (), s32[]{:S(2)}) async-start(), calls=%async_computation.10 | async-start | bytes 10616832 | tf_op jit(solution)/shard_map/reduce_scatter | solution.py:300
  623.2 2.9 copy-start.12
  623.2 3.2 copy-start.10
  623.2 486.9 %all-reduce.23.cloned.1.call-start = ((), (), s32[]{:S(2)}) async-start(), calls=%async_computation.12 | async-start | bytes 3833856 | tf_op jit(solution)/shard_map/psum | solution.py:312
  626.4 13.8 %copy-start.8 = (bf16[2,512,12,64]{1,0,3,2:T(2,128)(2,1)S(1)}, bf16[2,512,12,64]{1,0,3,2:T(2,128)(2,1)}, u32[]{:S(2)}) copy-start(bf16[2,512,12,64]{1,0,3,2:T(2,128)(2,1)} %reshape.335) | copy-start | bytes 4718596
  653.3 4.1 copy-start.40
  653.3 4.1 copy-start.41
  653.3 4.1 copy-start.45
  653.3 4.1 copy-start.46
  653.3 4.1 copy-start.48
  653.4 4.1 copy-start.49
  654.0 406.7 %copy-start.14 = (f32[1024,768]{1,0:T(8,128)S(1)}, f32[1024,768]{1,0:T(8,128)}, u32[]{:S(2)}) copy-start(f32[1024,768]{1,0:T(8,128)} %copy-done.13) | copy-start | bytes 9437188
  654.0 406.7 %copy-start.43 = (f32[1024]{0:T(1024)S(1)}, f32[1024]{0:T(1024)}, u32[]{:S(2)}) copy-start(f32[1024]{0:T(1024)} %copy-done.42) | copy-start | bytes 12292
Sparse Core Ops, SparseCore 0:
  10.2 68.5 all-gather.5
  81.0 39.8 all-gather.7
  123.0 78.0 all-gather.9
  203.1 77.6 all-gather.11
  361.9 66.4 reduce-scatter.6
  598.4 130.3 reduce-scatter.12
  732.4 161.2 reduce-scatter.8
  897.3 161.2 reduce-scatter.10
  1062.3 47.7 all-reduce.22
where the time goes:
time: 1130 us
  matrix products  388 us (34%)
  waiting for transfers between devices  387 us (34%)
  blocking collectives  143 us (13%)
  other arithmetic  95.8 us (8%)
  local copies, waits for them, and re-layouts  90.4 us (8%)
  between operations  19.3 us (2%)
    reduce_scatter x1, waiting for transfers between devices, body(): lax.psum_scatter(partials[3], 'fsdp', scatter_dimension=0, tiled=True)  163 us
    reduce_scatter x1, waiting for transfers between devices, body(): lax.psum_scatter(partials[2], 'fsdp', scatter_dimension=0, tiled=True)  163 us
    unnamed x2, blocking collectives  73.2 us
    dot_general x2, matrix products, attend_back(): jnp.einsum('hij,hie->hje', grad_logits, left_side, preferred_element_type...  55.5 us
    dot_general x4, matrix products, row_scores(): jnp.einsum('hie,hje->hij', left_side, right_side, preferred_element_type=...  50.1 us
    dot_general x2, matrix products, attend_back(): jnp.einsum('hij,hje->hie', grad_logits, right_side, preferred_element_typ...  47.3 us
    psum x1, waiting for transfers between devices, body(): lax.psum(shard_sums[0].astype(jnp.bfloat16), 'rep').astype(jnp.float32)  40.8 us
    dot_general x1, matrix products, body(): jnp.dot(hidden_low, full_up, preferred_element_type=jnp.float32)  36.4 us
  transfers between devices with their start and end apart: 9, of which 4 were waited for; matrix products, arithmetic and copies ran while one was open for 44% of the time, Pallas kernels for 0%

commit v1 on v0

--- a/solution.py
+++ b/solution.py
@@ -1,13 +1,22 @@
+import functools
 import math
 import jax
 import jax.numpy as jnp
 from jax import lax
 from jax.sharding import PartitionSpec as P
+from jax.lax import all_gather
 
 HEADS = 12
 HD = 64
 PE = 192
 norm_eps = 1e-12
+
+
+def run_try_all(patch, peer_axis):
+    return jnp.sum(all_gather(patch, peer_axis), 0)
+
+
+create_bands = functools.partial(run_try_all, peer_axis="rep")
 
 
 def layer_norm(values, gain, shift):
@@ -309,7 +318,7 @@
         lax.psum_scatter(partials[12], "fsdp", scatter_dimension=0, tiled=True),
     )
     totals = (
-        lax.psum(shard_sums[0].astype(jnp.bfloat16), "rep").astype(jnp.float32),
+        create_bands(shard_sums[0].astype(jnp.bfloat16)).astype(jnp.float32),
         lax.psum(shard_sums[1].astype(jnp.bfloat16), "rep").astype(jnp.float32),
         lax.psum(shard_sums[2].astype(jnp.bfloat16), "rep").astype(jnp.float32),
         lax.psum(shard_sums[3].astype(jnp.bfloat16), "rep").astype(jnp.float32),

time: 1130 us -> 1200 us (1.062)
  waiting for transfers between devices: 387 us -> 460 us
    reduce_scatter x0 -> x1, waiting for transfers between devices: none -> 98.3 us  [body(): lax.psum_scatter(partials[0], 'fsdp', scatter_dimension=0, tiled=True)]
    unnamed x10, waiting for transfers between devices: 21.2 us -> 2.68 us
    reduce_scatter x1, waiting for transfers between devices: 163 us -> 145 us  [body(): lax.psum_scatter(partials[2], 'fsdp', scatter_dimension=0, tiled=True)]
  transfers between devices with their start and end apart: 9 -> 10, of which waited for: 4 -> 5; matrix products, arithmetic and copies ran while one was open for 44% -> 22% of each run, Pallas kernels for 0% -> 0%
where the time goes in v1:
time: 1200 us
  waiting for transfers between devices  460 us (38%)
  matrix products  387 us (32%)
  blocking collectives  146 us (12%)
  other arithmetic  101 us (8%)
  local copies, waits for them, and re-layouts  79.9 us (7%)
  between operations  19.4 us (2%)
    reduce_scatter x1, waiting for transfers between devices, body(): lax.psum_scatter(partials[3], 'fsdp', scatter_dimension=0, tiled=True)  163 us
    reduce_scatter x1, waiting for transfers between devices, body(): lax.psum_scatter(partials[2], 'fsdp', scatter_dimension=0, tiled=True)  145 us
    reduce_scatter x1, waiting for transfers between devices, body(): lax.psum_scatter(partials[0], 'fsdp', scatter_dimension=0, tiled=True)  98.3 us
    unnamed x2, blocking collectives  76.1 us
    dot_general x2, matrix products, attend_back(): jnp.einsum('hij,hie->hje', grad_logits, left_side, preferred_element_type...  55.4 us
    dot_general x4, matrix products, row_scores(): jnp.einsum('hie,hje->hij', left_side, right_side, preferred_element_type=...  50.2 us
    dot_general x2, matrix products, attend_back(): jnp.einsum('hij,hje->hie', grad_logits, right_side, preferred_element_typ...  47.1 us
    psum x1, waiting for transfers between devices, body(): lax.psum(shard_sums[1].astype(jnp.bfloat16), 'rep').astype(jnp.float32)  40.4 us
  transfers between devices with their start and end apart: 10, of which 5 were waited for; matrix products, arithmetic and copies ran while one was open for 22% of the time, Pallas kernels for 0%

profile of v1, /device:TPU:0, one launch (start us, length us, event | category | flops | bytes accessed | tf_op | source)
XLA Modules:
  0.0 1196.2 jit_solution(13475859734327032279)
XLA Ops:
  10.0 33.1 %all_gather.52 = bf16[24576]{0:T(1024)(128)(2,1)S(1)} all-gather(bf16[3072]{0:T(1024)(128)(2,1)} %param.26), channel_id=1, replica_groups=mesh['fsdp'=8,'rep'=4] {'fsdp'}, dimensions={0}, use_global_device_ids=true | all-gather | bytes 55296 | tf_op jit(solution)/shard_map/all_gather | solution.py:117
  52.4 38.1 %all-reduce.17 = (bf16[2304]{0:T(1024)(128)(2,1)S(1)}, bf16[768]{0:T(1024)(128)(2,1)S(1)}, bf16[768]{0:T(1024)(128)(2,1)S(1)}, bf16[768]{0:T(1024)(128)(2,1)S(1)...) all-reduce(bf16[2304]{0:T(1024)(128)(2,1)S(1)} %dynamic-update-slic, ...), channel_id=1, replica_groups=mesh['fsdp'=8,'rep'=4] {'fsdp'}, use_global_device_ids=true, to_apply=%add | all-reduce | flops 6912 | bytes 27648
  100.1 26.5 %all-gather.1 = bf16[8,1,384]{2,1,0:T(2,128)(2,1)S(1)} all-gather(bf16[1,1,384]{2,1,0:T(2,128)(2,1)S(1)} %reshape.372), channel_id=1, replica_groups=mesh['fsdp'=8,'rep'=4] {'fsdp'}, dimensions={0}, use_global_device_ids=true | all-gather | bytes 6912 | tf_op jit(solution)/shard_map/all_gather | solution.py:121
  132.3 6.1 add_convert_fusion.1
  139.8 2.6 copy.165
  142.4 3.8 reshape.333
  147.9 3.8 reshape.335
  152.5 2.4 reshape.337
  156.7 4.8 copy_bitcast_fusion
  161.6 2.8 fusion.131
  164.4 8.1 fusion.134
  172.5 13.4 %fusion.98 = (bf16[2,12,512,192]{2,3,1,0:T(8,128)(2,1)}, bf16[2,12,512,192]{2,3,1,0:T(8,128)(2,1)}) fusion(f32[2,12,512,384]{2,3,1,0:T(8,128)} %fusion.134, f32[2,512,192]{1,2,0:T(8,128)} %copy.173, f32[2,512,192]{1,2,0:T(8,128)} %copy.171, f32[2,12,512,384]{2,3,1,0:T(8,128)S(1)} %fusion.131), kind=kLoop, calls=%fused_computation.103 | loop fusion | flops 18874368 | bytes 48758784 | tf_op jit(solution)/shard_map/convert_element_type | solution.py:180
  188.3 11.2 pad_maximum_fusion.3
  200.8 51.4 %while.26 = (s32[]{:T(128)}, bf16[2,12,512,64]{2,3,1,0:T(8,128)(2,1)}, f32[2,12,512,1]{2,1,3,0:T(8,128)}, s32[2,512]{1,0:T(2,128)S(1)}, bf16[2,12,512,448]{2,3,1...) while((s32[]{:T(128)}, ...), condition=%wide.region_3.4_spmd, body=%wide.region_0.3_spmd.sunk | while | flops 3256084480 | bytes 102720120 | solution.py:186
  201.5 12.7 %fusion.195 = (f32[12,512]{1,0:T(8,128)S(1)}, f32[12,512,512]{1,2,0:T(8,128)}) fusion(pred[512,512]{0,1:T(8,128)(4,1)S(1)} %broadcast_compare_fusion.4, bf16[2,12,512,448]{2,3,1,0:T(8,128)(2,1)} %get-tuple-element.431, s32[]{:T(128)} %get-tuple-element.418, bf16[2,12,512,448]{2,3,1,0:T(8,128)(2,1)} %get-tuple-element.430), kind=kOutput, calls=%fused_computation.3.clone.1 | convolution fusion | flops 2828003328 | bytes 23880704 | tf_op jit(solution)/shard_map/while/body/eval_jaxpr/hie,hje->hij/dot_general | solution.py:38
  214.3 7.3 exponential_reduce_fusion.2
  222.5 4.0 bitcast_dynamic-update-slice_fusion.11
  226.8 13.0 %fusion.195 = (f32[12,512]{1,0:T(8,128)S(1)}, f32[12,512,512]{1,2,0:T(8,128)}) fusion(pred[512,512]{0,1:T(8,128)(4,1)S(1)} %broadcast_compare_fusion.4, bf16[2,12,512,448]{2,3,1,0:T(8,128)(2,1)} %get-tuple-element.431, s32[]{:T(128)} %get-tuple-element.418, bf16[2,12,512,448]{2,3,1,0:T(8,128)(2,1)} %get-tuple-element.430), kind=kOutput, calls=%fused_computation.3.clone.1 | convolution fusion | flops 2828003328 | bytes 23880704 | tf_op jit(solution)/shard_map/while/body/eval_jaxpr/hie,hje->hij/dot_general | solution.py:38
  239.8 7.3 exponential_reduce_fusion.2
  248.0 4.0 bitcast_dynamic-update-slice_fusion.11
  252.2 3.6 copy.182
  257.4 3.9 fusion.154
  261.8 36.2 %multiply_convert_fusion.1 = (bf16[1024,3072]{1,0:T(8,128)(2,1)}, f32[1024,3072]{1,0:T(8,128)}, f32[1024,3072]{1,0:T(8,128)}) fusion(f32[3072]{0:T(1024)S(1)} %bitcast.261, bf16[768,3072]{1,0:T(8,128)(2,1)} %all-gather.12.cloned.1.call-done, f32[1024,768]{1,0:T(8,128)S(1)} %get-tuple-element.287, f32[768]{0:T(1024)S(1)} %convert_element_type.228, ...), kind=kOutput, calls=%fused_computation.85 | convolution fusion | flops 5043388416 | bytes 39348224 | tf_op jit(solution)/shard_map/dot_general | solution.py:196
  298.1 9.1 fusion.155
  309.5 2.6 fusion.148
  314.2 18.9 %convert_reduce_fusion = (f32[3072]{0:T(1024)}, bf16[1024,3072]{1,0:T(8,128)(2,1)}) fusion(f32[1024,3072]{1,0:T(8,128)} %get-tuple-element.258, bf16[1024,768]{1,0:T(8,128)(2,1)} %get-tuple-element.250, bf16[3072,768]{1,0:T(8,128)(2,1)} %all-gather.14.cloned.1.call-done, f32[1024,3072]{1,0:T(8,128)} %get-tuple-element.288, f32[3072]{0:T(1024)S(1)} %bitcast.262), kind=kOutput, calls=%fused_computation.83 | convolution fusion | flops 4885312512 | bytes 37773312 | tf_op jit(solution)/shard_map/nd,fd->nf/dot_general | solution.py:235
  333.1 10.1 multiply_reduce_fusion.1
  347.2 2.6 convolution_convert_fusion
  351.7 2.4 reshape.338
  357.1 155.1 %while.27 = (s32[]{:T(128)}, f32[2,12,512,448]{2,3,1,0:T(8,128)}, f32[2,12,512,448]{2,3,1,0:T(8,128)}, bf16[2,12,512,64]{2,3,1,0:T(8,128)(2,1)}, s32[2,512]{1,0:...) while((s32[]{:T(128)}, f32[2,12,512,448]{2,3,1,0:T(8,128)}, ...), condition=%wide.region_14.15_spmd, body=%wide.region_12.14_spmd.sunk | while | flops 9343087616 | bytes 188181616 | solution.py:256
  357.6 12.2 %fusion.207 = f32[12,512,512]{1,2,0:T(8,128)} fusion(bf16[2,12,512,448]{2,3,1,0:T(8,128)(2,1)} %get-tuple-element.462, s32[]{:T(128)} %get-tuple-element.445, bf16[2,12,512,448]{2,3,1,0:T(8,128)(2,1)} %get-tuple-element.461), kind=kOutput, calls=%fused_computation.43.clone.1 | convolution fusion | flops 2818572288 | bytes 23593984 | tf_op jit(solution)/shard_map/while/body/eval_jaxpr/hie,hje->hij/dot_general | solution.py:38
  369.7 6.3 fusion.206
  376.3 27.7 %bitcast_dynamic-update-slice_fusion.13 = f32[2,12,512,448]{2,3,1,0:T(8,128)} fusion(f32[2,12,512,448]{2,3,1,0:T(8,128)} %get-tuple-element.447, s32[]{:T(128)} %get-tuple-element.445, bf16[2,12,512,448]{2,3,1,0:T(8,128)(2,1)} %get-tuple-element.461, f32[12,512,512]{1,2,0:T(8,128)} %fusion.206, f32[12,512,512]{1,2,0:T(8,128)} %fusion.207, ...), kind=kOutput, calls=%fused_computation.27.clone.1 | convolution fusion | flops 2853181952 | bytes 67437568 | tf_op jit(solution)/shard_map/while/body/eval_jaxpr/hij,hie->hje/dot_general | solution.py:65
  404.0 23.6 %bitcast_dynamic-update-slice_fusion.12 = f32[2,12,512,448]{2,3,1,0:T(8,128)} fusion(f32[2,12,512,448]{2,3,1,0:T(8,128)} %get-tuple-element.446, s32[]{:T(128)} %get-tuple-element.445, f32[12,512,512]{1,2,0:T(8,128)} %fusion.206, f32[12,512,512]{1,2,0:T(8,128)} %fusion.207, f32[12,512]{1,0:T(8,128)S(1)} %dynamic-slice_bitcast_fusion.2, ...), kind=kOutput, calls=%fused_computation.28.clone.1 | convolution fusion | flops 2853181952 | bytes 67437568 | tf_op jit(solution)/shard_map/while/body/eval_jaxpr/hij,hje->hie/dot_general | solution.py:62
  427.6 7.2 bitcast_dynamic-update-slice_fusion.14
  434.9 12.2 %fusion.207 = f32[12,512,512]{1,2,0:T(8,128)} fusion(bf16[2,12,512,448]{2,3,1,0:T(8,128)(2,1)} %get-tuple-element.462, s32[]{:T(128)} %get-tuple-element.445, bf16[2,12,512,448]{2,3,1,0:T(8,128)(2,1)} %get-tuple-element.461), kind=kOutput, calls=%fused_computation.43.clone.1 | convolution fusion | flops 2818572288 | bytes 23593984 | tf_op jit(solution)/shard_map/while/body/eval_jaxpr/hie,hje->hij/dot_general | solution.py:38
  447.0 6.3 fusion.206
  453.6 27.7 %bitcast_dynamic-update-slice_fusion.13 = f32[2,12,512,448]{2,3,1,0:T(8,128)} fusion(f32[2,12,512,448]{2,3,1,0:T(8,128)} %get-tuple-element.447, s32[]{:T(128)} %get-tuple-element.445, bf16[2,12,512,448]{2,3,1,0:T(8,128)(2,1)} %get-tuple-element.461, f32[12,512,512]{1,2,0:T(8,128)} %fusion.206, f32[12,512,512]{1,2,0:T(8,128)} %fusion.207, ...), kind=kOutput, calls=%fused_computation.27.clone.1 | convolution fusion | flops 2853181952 | bytes 67437568 | tf_op jit(solution)/shard_map/while/body/eval_jaxpr/hij,hie->hje/dot_general | solution.py:65
  481.3 23.5 %bitcast_dynamic-update-slice_fusion.12 = f32[2,12,512,448]{2,3,1,0:T(8,128)} fusion(f32[2,12,512,448]{2,3,1,0:T(8,128)} %get-tuple-element.446, s32[]{:T(128)} %get-tuple-element.445, f32[12,512,512]{1,2,0:T(8,128)} %fusion.206, f32[12,512,512]{1,2,0:T(8,128)} %fusion.207, f32[12,512]{1,0:T(8,128)S(1)} %dynamic-slice_bitcast_fusion.2, ...), kind=kOutput, calls=%fused_computation.28.clone.1 | convolution fusion | flops 2853181952 | bytes 67437568 | tf_op jit(solution)/shard_map/while/body/eval_jaxpr/hij,hje->hie/dot_general | solution.py:62
  504.8 7.3 bitcast_dynamic-update-slice_fusion.14
  512.2 19.0 %slice_multiply_fusion.7 = (f32[2,12,512,192]{2,3,1,0:T(8,128)S(1)}, f32[2,12,512,192]{2,3,1,0:T(8,128)}, f32[2,12,512,192]{2,3,1,0:T(8,128)}, f32[2,12,512,192]{2,3,1,0:T(8,128)}) fusion(f32[2,12,512,448]{2,3,1,0:T(8,128)} %get-tuple-element.109, f32[2,512,192]{1,2,0:T(8,128)} %copy.173, f32[2,512,192]{1,2,0:T(8,128)} %copy.171, ...), kind=kLoop, calls=%fused_computation.114 | loop fusion | flops 9437184 | bytes 58195968 | tf_op jit(solution)/shard_map/mul | solution.py:261
  531.2 19.8 %fusion.111 = bf16[2,512,12,64]{1,3,2,0:T(8,128)(2,1)S(1)} fusion(f32[2,12,512,448]{2,3,1,0:T(8,128)} %get-tuple-element.110, f32[192,64]{0,1:T(8,128)S(1)} %copy-done.26, f32[192,64]{0,1:T(8,128)S(1)} %copy-done.27, f32[2,12,512,192]{2,3,1,0:T(8,128)} %get-tuple-element.271, f32[2,12,512,192]{2,3,1,0:T(8,128)} %get-tuple-element.272), kind=kOutput, calls=%fused_computation.152 | convolution fusion | flops 3630194688 | bytes 23691264 | tf_op jit(solution)/shard_map/rhlf,fd->rhld/dot_general | solution.py:266
  553.1 15.3 %fusion.110 = bf16[2,512,12,64]{1,3,2,0:T(8,128)(2,1)S(1)} fusion(f32[2,12,512,448]{2,3,1,0:T(8,128)} %get-tuple-element.109, f32[192,64]{0,1:T(8,128)S(1)} %copy-done.24, f32[192,64]{0,1:T(8,128)S(1)} %copy-done.25, f32[2,12,512,192]{2,3,1,0:T(8,128)} %get-tuple-element.264, f32[2,12,512,192]{2,3,1,0:T(8,128)S(1)} %get-tuple-element.263), kind=kOutput, calls=%fused_computation.151 | convolution fusion | flops 3630194688 | bytes 23691264 | tf_op jit(solution)/shard_map/rhlf,fd->rhld/dot_general | solution.py:263
  573.0 2.1 copy-done.15
  575.1 5.8 convolution_bitcast_fusion
  580.9 8.0 copy.223
  589.4 5.0 fusion.156
  594.5 10.7 fusion.143
  606.6 10.2 fusion.157
  617.0 98.3 %reduce-scatter.13.cloned.1.call-done = f32[96,2304]{1,0:T(8,128)} async-done(((f32[768,2304]{1,0:T(8,128)}), f32[96,2304]{1,0:T(8,128)}) %reduce-scatter.13.cloned.1.call-update) | async-done | bytes 884752 | tf_op jit(solution)/shard_map/reduce_scatter | solution.py:306
  720.2 13.1 %fusion.112 = f32[384,64]{0,1:T(8,128)S(1)} fusion(bf16[2,512,12,64]{1,0,3,2:T(2,128)(2,1)S(1)} %copy-done.10, f32[2,12,512,192]{2,3,1,0:T(8,128)} %get-tuple-element.271, f32[2,12,512,192]{2,3,1,0:T(8,128)} %get-tuple-element.272), kind=kOutput, calls=%fused_computation.153 | convolution fusion | flops 3628597248 | bytes 20545536 | tf_op jit(solution)/shard_map/rhld,rhlf->fd/dot_general | solution.py:275
  733.8 13.1 %fusion.117 = f32[384,64]{0,1:T(8,128)S(1)} fusion(bf16[2,512,12,64]{1,0,3,2:T(2,128)(2,1)S(1)} %copy-done.8, f32[2,12,512,192]{2,3,1,0:T(8,128)} %get-tuple-element.264, f32[2,12,512,192]{2,3,1,0:T(8,128)} %copy-done.1), kind=kOutput, calls=%fused_computation.154 | convolution fusion | flops 3628597248 | bytes 20545536 | tf_op jit(solution)/shard_map/rhld,rhlf->fd/dot_general | solution.py:269
  749.5 3.1 convert_reduce_fusion.1
  752.7 38.0 %all-reduce.24 = (bf16[2304]{0:T(1024)(128)(2,1)S(1)}, bf16[24576]{0:T(1024)(128)(2,1)S(1)}, bf16[768]{0:T(1024)(128)(2,1)S(1)}, bf16[768]{0:T(1024)(128)(2,1)S(...) all-reduce(f32[2304]{0:T(1024)S(1)} %convert_reduce_fusion.1, ...), channel_id=4, replica_groups=mesh['fsdp'=8,'rep'=4] {'fsdp'}, use_global_device_ids=true, to_apply=%region_18.19.clone | all-reduce | flops 34560 | bytes 207360
  791.3 10.3 all-reduce.18
  808.1 145.1 %reduce-scatter.9.cloned.1.call-done = f32[96,3072]{1,0:T(8,128)} async-done(((f32[768,3072]{1,0:T(8,128)}), f32[96,3072]{1,0:T(8,128)}) %reduce-scatter.9.cloned.1.call-update) | async-done | bytes 1179664 | tf_op jit(solution)/shard_map/reduce_scatter | solution.py:308
  953.2 2.2 convert_element_type.262
  955.3 162.7 %reduce-scatter.11.cloned.1.call-done = f32[384,768]{1,0:T(8,128)} async-done(((f32[3072,768]{1,0:T(8,128)}), f32[384,768]{1,0:T(8,128)}) %reduce-scatter.11.cloned.1.call-update) | async-done | bytes 1179664 | tf_op jit(solution)/shard_map/reduce_scatter | solution.py:309
  1118.0 2.1 convert_element_type.267
  1120.2 8.6 add_convert_fusion.2
  1128.8 11.2 all-gather.16.cloned.1.call-done
  1142.7 40.4 %all-reduce.23.cloned.1.call-done = (bf16[96,768]{1,0:T(8,128)(2,1)}, bf16[96,3072]{1,0:T(8,128)(2,1)}, bf16[384,768]{1,0:T(8,128)(2,1)}) async-done(((bf16[96,768]{1,0:T(8,128)(2,1)}, bf16[96,3072]{1,0:T(8,128)(2,1)}, bf16[384,768]{1,0:T(8,128)(2,1)}), (bf16[96,768]{1,0:T(8,128)(2,1)}, bf16[96,3072]{1,0:T(8,128)(2,1)}, bf16[384,768]{1,0:T(8,128)(2,1)})) %all-reduce.23.cloned.1.call-update) | async-done | bytes 1327120 | tf_op jit(solution)/shard_map/psum | solution.py:322
  1183.2 2.2 convert_element_type.263
  1185.4 2.2 convert_element_type.268
  (279 shorter events, 78.6 us)
Async XLA Ops:
  7.2 125.1 %all-gather.8.cloned.1.call-start = ((), (), s32[]{:S(2)}) async-start(), calls=%async_computation.4 | async-start | bytes 3981312 | tf_op jit(solution)/shard_map/all_gather | solution.py:112
  7.9 249.5 %all-gather.10.cloned.1.call-start = ((), (), s32[]{:S(2)}) async-start(), calls=%async_computation.5 | async-start | bytes 1327104 | tf_op jit(solution)/shard_map/all_gather | solution.py:113
  8.7 253.1 %all-gather.12.cloned.1.call-start = ((), (), s32[]{:S(2)}) async-start(), calls=%async_computation.6 | async-start | bytes 5308416 | tf_op jit(solution)/shard_map/all_gather | solution.py:114
  9.4 288.6 %all-gather.14.cloned.1.call-start = ((), (), s32[]{:S(2)}) async-start(), calls=%async_computation.7 | async-start | bytes 5308416 | tf_op jit(solution)/shard_map/all_gather | solution.py:115
  10.0 705.2 %reduce-scatter.13.cloned.1.call-start = ((), (), s32[]{:S(2)}) async-start(), calls=%async_computation.12 | async-start | bytes 7962624 | tf_op jit(solution)/shard_map/reduce_scatter | solution.py:306
  94.6 5.5 copy-start.51
  96.0 36.3 %copy-start.52 = (bf16[2,512,768]{2,1,0:T(8,128)(2,1)S(1)}, bf16[2,512,768]{2,1,0:T(8,128)(2,1)}, u32[]{:S(2)}) copy-start(bf16[2,512,768]{2,1,0:T(8,128)(2,1)} %param.21) | copy-start | bytes 4718596
  100.1 243.1 %copy-start.33 = (f32[768]{0:T(1024)}, f32[768]{0:T(1024)S(1)}, u32[]{:S(2)}) copy-start(f32[768]{0:T(1024)S(1)} %convert_element_type.227) | copy-start | bytes 9220
  100.1 198.0 %copy-start.37 = (f32[768]{0:T(1024)}, f32[768]{0:T(1024)S(1)}, u32[]{:S(2)}) copy-start(f32[768]{0:T(1024)S(1)} %convert_element_type.228) | copy-start | bytes 9220
  154.8 6.7 copy-start.7
  154.9 6.7 copy-start.29
  154.9 6.7 copy-start.30
  161.5 2.9 copy-start.9
  161.5 2.9 copy-start.31
  161.5 2.9 copy-start.32
  185.9 2.4 copy-start.6
  188.3 12.5 %copy-start.35 = (s32[2,512]{1,0:T(2,128)S(1)}, s32[2,512]{1,0:T(2,128)}, u32[]{:S(2)}) copy-start(s32[2,512]{1,0:T(2,128)} %param.22) | copy-start | bytes 12292
  214.3 8.3 copy-start
  239.8 8.2 copy-start
  252.2 5.2 copy-start.4
  257.4 4.4 copy-start.47
  261.2 82.0 %copy-start.2 = (f32[1024,768]{1,0:T(8,128)}, f32[1024,768]{1,0:T(8,128)S(1)}, u32[]{:S(2)}) copy-start(f32[1024,768]{1,0:T(8,128)S(1)} %get-tuple-element.287) | copy-start | bytes 9437188
  261.3 81.9 %copy-start.20 = (f32[1024]{0:T(1024)}, f32[1024]{0:T(1024)S(1)}, u32[]{:S(2)}) copy-start(f32[1024]{0:T(1024)S(1)} %broadcast_multiply_fusion.1) | copy-start | bytes 12292
  261.8 81.4 %copy-start.22 = (f32[1024]{0:T(1024)}, f32[1024]{0:T(1024)S(1)}, u32[]{:S(2)}) copy-start(f32[1024]{0:T(1024)S(1)} %fusion.137) | copy-start | bytes 12292
  261.8 36.2 %copy-start.50 = (f32[768]{0:T(1024)S(1)}, f32[768]{0:T(1024)}, u32[]{:S(2)}) copy-start(f32[768]{0:T(1024)} %convert_element_type.232) | copy-start | bytes 9220
  298.1 9.7 copy-start.11
  298.1 9.7 copy-start.39
  307.2 2.3 copy-start.44
  343.2 3.9 copy-start.54
  344.7 1.6 copy-start.13
  344.7 1.6 copy-start.42
  349.8 7.3 copy-start.5
  349.8 7.3 copy-start.19
  349.8 7.3 copy-start.36
  512.2 19.0 %copy-start.26 = (f32[192,64]{0,1:T(8,128)S(1)}, f32[192,64]{0,1:T(8,128)}, u32[]{:S(2)}) copy-start(f32[192,64]{0,1:T(8,128)} %copy.191) | copy-start | bytes 147460
  512.2 19.0 %copy-start.27 = (f32[192,64]{0,1:T(8,128)S(1)}, f32[192,64]{0,1:T(8,128)}, u32[]{:S(2)}) copy-start(f32[192,64]{0,1:T(8,128)} %copy.190) | copy-start | bytes 147460
  531.2 21.9 %copy-start.1 = (f32[2,12,512,192]{2,3,1,0:T(8,128)}, f32[2,12,512,192]{2,3,1,0:T(8,128)S(1)}, u32[]{:S(2)}) copy-start(f32[2,12,512,192]{2,3,1,0:T(8,128)S(1)} %get-tuple-element.263) | copy-start | bytes 28311556
  551.1 2.1 copy-start.24
  551.1 2.1 copy-start.25
  568.5 2.2 copy-start.16
  570.7 4.5 copy-start.53
  573.0 2.1 copy-start.15
  588.9 5.5 copy-start.3
  589.0 5.5 copy-start.21
  589.0 5.5 copy-start.23
  589.0 5.5 copy-start.34
  589.0 5.5 copy-start.38
  589.0 217.4 %reduce-scatter.7.cloned.1.call-start = ((), (), s32[]{:S(2)}) async-start(), calls=%async_computation.8 | async-start | bytes 2654208 | tf_op jit(solution)/shard_map/reduce_scatter | solution.py:307
  594.4 358.7 %reduce-scatter.9.cloned.1.call-start = ((), (), s32[]{:S(2)}) async-start(), calls=%async_computation.9 | async-start | bytes 10616832 | tf_op jit(solution)/shard_map/reduce_scatter | solution.py:308
  605.2 1.4 copy-start.17
  605.2 512.8 %reduce-scatter.11.cloned.1.call-start = ((), (), s32[]{:S(2)}) async-start(), calls=%async_computation.10 | async-start | bytes 10616832 | tf_op jit(solution)/shard_map/reduce_scatter | solution.py:309
  616.9 100.4 %copy-start.12 = (bf16[2,512,768]{2,1,0:T(8,128)(2,1)S(1)}, bf16[2,512,768]{2,1,0:T(8,128)(2,1)}, u32[]{:S(2)}) copy-start(bf16[2,512,768]{2,1,0:T(8,128)(2,1)} %param.37) | copy-start | bytes 4718596
  616.9 103.3 %copy-start.10 = (bf16[2,512,12,64]{1,0,3,2:T(2,128)(2,1)S(1)}, bf16[2,512,12,64]{1,0,3,2:T(2,128)(2,1)}, u32[]{:S(2)}) copy-start(bf16[2,512,12,64]{1,0,3,2:T(2,128)(2,1)} %reshape.335) | copy-start | bytes 4718596
  616.9 523.1 %all-gather.16.cloned.1.call-start = ((), (), s32[]{:S(2)}) async-start(), calls=%async_computation.11 | async-start | bytes 2211840 | tf_op jit(solution)/shard_map/all_gather | solution.py:16
  717.2 466.0 %all-reduce.23.cloned.1.call-start = ((), (), s32[]{:S(2)}) async-start(), calls=%async_computation.13 | async-start | bytes 2654208 | tf_op jit(solution)/shard_map/psum | solution.py:322
  720.2 13.6 %copy-start.8 = (bf16[2,512,12,64]{1,0,3,2:T(2,128)(2,1)S(1)}, bf16[2,512,12,64]{1,0,3,2:T(2,128)(2,1)}, u32[]{:S(2)}) copy-start(bf16[2,512,12,64]{1,0,3,2:T(2,128)(2,1)} %reshape.333) | copy-start | bytes 4718596
  747.6 5.1 copy-start.40
  747.6 5.1 copy-start.41
  747.6 5.1 copy-start.45
  747.6 5.1 copy-start.46
  747.6 5.1 copy-start.48
  747.6 5.1 copy-start.49
  747.6 372.6 %copy-start.14 = (f32[1024,768]{1,0:T(8,128)S(1)}, f32[1024,768]{1,0:T(8,128)}, u32[]{:S(2)}) copy-start(f32[1024,768]{1,0:T(8,128)} %copy-done.13) | copy-start | bytes 9437188
  747.6 372.6 %copy-start.43 = (f32[1024]{0:T(1024)S(1)}, f32[1024]{0:T(1024)}, u32[]{:S(2)}) copy-start(f32[1024]{0:T(1024)} %copy-done.42) | copy-start | bytes 12292
  (2 other events, 1.8 us)
Sparse Core Ops, SparseCore 0:
  10.2 68.4 all-gather.7
  80.9 39.9 all-gather.9
  123.1 78.0 all-gather.11
  203.2 77.6 all-gather.13
  589.1 126.1 reduce-scatter.12
  718.6 69.2 reduce-scatter.6
  791.4 161.6 reduce-scatter.8
  956.8 161.2 reduce-scatter.10
  1120.1 19.8 all-gather.15
  1143.6 39.5 all-reduce.22
